TPU v7x, 32 devices: a whole 2x2x4 slice. The times are simulated.
32 devices in a mesh: chan: 4 (over x, core), az: 2 (over y), rng: 4 (over z).
Axes of the slice: x: 2, y: 2, z: 4, core: 2. Of those that a mesh axis runs over, the one named last changes fastest.
Arguments:
- raw: float32 [2, 16, 64, 16384], P(None, 'chan', 'rng', 'az'), may hold values from -6 to 6
- taps: float32 [2, 17, 64], P(None, None, 'rng'), may hold values from -1.5 to 1.5
- recon: float32 [2, 16, 16, 16384], P(None, 'az', None, ('chan', 'rng')), may hold values from -1 to 1
- channel_slot: int32 [16], replicated, may hold values from 0 to 15, each once
Outputs:
- reconstructed: float32 [2, 16, 4, 16, 16384], P(None, None, None, 'az', ('chan', 'rng'))
Inputs may be any that keep to these rules, and one draw needn't show every extreme that they name: `channel_slot`: a permutation of the channels.
All inputs are finite; a program needn't handle non-finite values.
Results may differ from a plain program's by a relative error of at most 0.0003.
Values sent between devices are 32-bit elements; how exact they have to be, the bound alone decides.
No kernel may reach another device: no remote copies, remote signals or barrier semaphores. Data moves between devices by JAX's collectives and lax.ppermute only.
A program may use at most 192 MiB of HBM per device.

v0:
```python
import math
import jax
import jax.numpy as jnp
from jax import lax
from jax.sharding import PartitionSpec as P


def with_halo(shard, sides, width):
    for axis, dim in sides:
        size, length = (lax.axis_size(axis), shard.shape[dim])
        up = [(i, (i + 1) % size) for i in range(size - 1)]
        down = [(j, i) for i, j in up]
        last = lax.slice_in_dim(shard, length - width, length, axis=dim)
        leading = lax.slice_in_dim(shard, 0, width, axis=dim)
        before = lax.ppermute(last, axis, up)
        after = lax.ppermute(leading, axis, down)
        shard = jnp.concatenate([before, shard, after], axis=dim)
    return shard


def phases(first, second, length):
    left = jnp.arange(first, dtype=jnp.int32)
    right = jnp.arange(second, dtype=jnp.int32)
    product = left[:, None] * right[None, :] % length
    angle = product.astype(jnp.float32) * (2.0 * math.pi / length)
    return (jnp.cos(angle), jnp.sin(angle))


def azimuth_fft(block):
    count = block.shape[-1]
    rows = math.isqrt(count)
    while count % rows:
        rows = rows - 1
    cols = count // rows
    lead = block.shape[1:-1]
    high = lax.Precision.HIGHEST
    real_in = block[0].reshape(lead + (rows, cols))
    imag_in = block[1].reshape(lead + (rows, cols))
    cosine_first, sine_first = phases(rows, rows, rows)
    first_real = jnp.einsum("...ab,af->...bf", real_in, cosine_first, precision=high) + jnp.einsum(
        "...ab,af->...bf", imag_in, sine_first, precision=high
    )
    first_imag = jnp.einsum("...ab,af->...bf", imag_in, cosine_first, precision=high) - jnp.einsum(
        "...ab,af->...bf", real_in, sine_first, precision=high
    )
    twist_cos, twist_sin = phases(cols, rows, count)
    turned_real = first_real * twist_cos + first_imag * twist_sin
    turned_imag = first_imag * twist_cos - first_real * twist_sin
    cosine_second, sine_second = phases(cols, cols, cols)
    out_real = jnp.einsum(
        "...bf,bg->...gf", turned_real, cosine_second, precision=high
    ) + jnp.einsum("...bf,bg->...gf", turned_imag, sine_second, precision=high)
    out_imag = jnp.einsum(
        "...bf,bg->...gf", turned_imag, cosine_second, precision=high
    ) - jnp.einsum("...bf,bg->...gf", turned_real, sine_second, precision=high)
    scale = 1.0 / math.sqrt(count)
    return jnp.stack([out_real.reshape(lead + (count,)), out_imag.reshape(lead + (count,))]) * scale


def shards(raw, taps, recon, channel_slot):
    width = taps.shape[1]
    half = (width - 1) // 2
    strip_rows = raw.shape[2]
    padded = with_halo(raw, (("rng", 2),), half)
    real_part = jnp.zeros(raw.shape[1:], jnp.float32)
    imag_part = jnp.zeros(raw.shape[1:], jnp.float32)
    for offset in range(width):
        seg_real = padded[0, :, offset : offset + strip_rows, :]
        seg_imag = padded[1, :, offset : offset + strip_rows, :]
        tap_real = taps[0, offset][None, :, None]
        tap_imag = taps[1, offset][None, :, None]
        real_part = real_part + tap_real * seg_real - tap_imag * seg_imag
        imag_part = imag_part + tap_real * seg_imag + tap_imag * seg_real
    filtered = jnp.stack([real_part, imag_part])
    spectrum = azimuth_fft(lax.all_to_all(filtered, "az", split_axis=2, concat_axis=3, tiled=True))
    strips = lax.axis_size("rng")
    groups = lax.axis_size("chan")
    local_channels = spectrum.shape[1]
    local_range = spectrum.shape[2]
    moved = lax.all_to_all(
        spectrum[:, None], ("chan", "rng"), split_axis=4, concat_axis=1, tiled=True
    )
    bins = moved.shape[-1]
    moved = moved.reshape((2, groups, strips, local_channels, local_range, bins))
    doppler = jnp.transpose(moved, (0, 1, 3, 2, 4, 5)).reshape(
        (2, groups * local_channels, strips * local_range, bins)
    )
    channels = doppler.shape[1]
    selector = (channel_slot[:, None] == jnp.arange(channels, dtype=jnp.int32)[None, :]).astype(
        jnp.float32
    )
    piece = lax.all_gather(recon, "az", axis=1, tiled=True)
    arranged = jnp.einsum("pkjf,cj->pkcf", piece, selector, precision=lax.Precision.HIGHEST)
    shape = (piece.shape[1], doppler.shape[2], doppler.shape[3])
    out_real = jnp.zeros(shape, jnp.float32)
    out_imag = jnp.zeros(shape, jnp.float32)
    for channel in range(channels):
        mat_real = arranged[0, :, channel, None, :]
        mat_imag = arranged[1, :, channel, None, :]
        data_real = doppler[0, channel][None]
        data_imag = doppler[1, channel][None]
        out_real = out_real + mat_real * data_real - mat_imag * data_imag
        out_imag = out_imag + mat_real * data_imag + mat_imag * data_real
    result = jnp.stack([out_real, out_imag])
    total_range = result.shape[2]
    return result.reshape((2, result.shape[1], strips, total_range // strips, result.shape[3]))


def solution(mesh):
    return jax.shard_map(
        shards,
        mesh=mesh,
        in_specs=(
            P(None, "chan", "rng", "az"),
            P(None, None, "rng"),
            P(None, "az", None, ("chan", "rng")),
            P(),
        ),
        out_specs=P(None, None, None, "az", ("chan", "rng")),
        check_vma=False,
    )
```

profile of v0, /device:TPU:0, one launch (start us, length us, event | category | flops | bytes accessed | tf_op | source)
XLA Modules:
  0.0 701.0 jit_solution(1237962557530691339)
XLA Ops:
  6.5 2.5 fusion.71
  9.0 5.1 collective-permute-start
  14.1 1.3 collective-permute-start.1
  15.5 0.5 slice_reduce_fusion.33
  15.9 0.4 slice_reduce_fusion.32
  16.4 42.5 %collective-permute-done = f32[2,4,8,8192]{3,2,1,0:T(8,128)S(1)} collective-permute-done((f32[2,4,8,8192]{3,2,1,0:T(8,128)S(1)}, f32[2,4,8,8192]{3,2,1,0:T(8,128)S(1)}, u32[]{:S(2)}, u32[]{:S(2)}) %collective-permute-start) | collective-permute-done | bytes 2097184 | tf_op jit(solution)/shard_map/ppermute | solution.py:15
  58.9 1.5 constant_dynamic-update-slice_fusion.1
  60.4 4.2 constant_dynamic-update-slice_fusion
  64.6 1.5 constant_dynamic-update-slice_fusion.2
  66.1 44.7 %multiply_subtract_fusion.2 = f32[1,4,16,8192]{3,2,1,0:T(8,128)} fusion(f32[2,4,24,8192]{3,2,1,0:T(8,128)} %constant_dynamic-update-slice_fusion.2, f32[2,4,24,8192]{3,2,1,0:T(8,128)} %get-tuple-element.73, f32[2,4,16,8192]{3,2,1,0:T(8,128)S(1)} %copy-done, f32[16]{0:T(128)S(1)} %get-tuple-element.37, f32[16]{0:T(128)S(1)} %get-tuple-element.38, ...), kind=kLoop, calls=%fused_computation.11 | loop fusion | flops 35127296 | bytes 73402496 | tf_op jit(solution)/shard_map/sub | solution.py:72
  110.8 44.8 %multiply_add_fusion.2 = f32[1,4,16,8192]{3,2,1,0:T(8,128)} fusion(f32[2,4,24,8192]{3,2,1,0:T(8,128)} %constant_dynamic-update-slice_fusion.2, f32[2,4,24,8192]{3,2,1,0:T(8,128)} %get-tuple-element.73, f32[2,4,16,8192]{3,2,1,0:T(8,128)S(1)} %copy-done, f32[16]{0:T(128)S(1)} %get-tuple-element.37, f32[16]{0:T(128)S(1)} %get-tuple-element.38, ...), kind=kLoop, calls=%fused_computation.10 | loop fusion | flops 35127296 | bytes 73402496 | tf_op jit(solution)/shard_map/add | solution.py:73
  155.5 2.5 pad_maximum_fusion
  158.1 4.7 copy.126
  162.8 5.8 all-to-all-start
  168.9 0.3 fusion.23
  169.3 46.1 %all-to-all-done = f32[2,4,16,8192]{3,1,0,2:T(4,128)} async-done(((f32[2,4,16,8192]{3,1,0,2:T(4,128)}), f32[2,4,16,8192]{3,1,0,2:T(4,128)}, u32[]{:S(2)}, u32[]{:S(2)}) %all-to-all-start) | async-done | bytes 4194336 | tf_op jit(solution)/shard_map/all_to_all | solution.py:75
  215.4 5.4 copy.224
  220.8 2.3 fusion.70
  223.1 3.1 reshape_squeeze.7
  226.1 4.9 fusion.6
  231.0 4.2 reshape_squeeze.6
  235.2 5.4 fusion.8
  240.6 3.7 convolution_subtract_fusion
  244.3 3.6 convolution_add_fusion
  247.9 2.7 fusion
  250.6 3.5 fusion.1
  254.1 3.7 add_bitcast_fusion
  257.8 2.7 stack.18
  260.5 5.8 subtract_bitcast_fusion
  266.3 2.9 stack.19
  269.2 3.9 maximum_multiply_fusion
  273.1 44.6 %copy.138 = f32[2,1,4,8,16384]{3,2,1,0,4:T(4,128)} copy(f32[2,1,4,8,16384]{4,3,2,1,0:T(8,128)} %maximum_multiply_fusion) | data formatting | bytes 8388608 | tf_op jit(solution)/shard_map/mul | solution.py:57
  317.7 82.5 %reshape.729 = f32[16,1,65536]{2,1,0:T(1,128)} reshape(f32[16384,2,1,4,8]{4,3,2,1,0:T(4,128)} %bitcast.180) | data formatting | bytes 8388608
  400.3 7.0 all-to-all-start.1
  407.3 0.7 all-gather.2.cloned.1.call-update
  408.0 35.1 %all-gather.2.cloned.1.call-done = f32[2,16,16,1024]{3,2,1,0:T(8,128)} async-done(((f32[2,8,16,1024]{3,2,1,0:T(8,128)}), f32[2,16,16,1024]{3,2,1,0:T(8,128)}) %all-gather.2.cloned.1.call-update) | async-done | bytes 2097168 | tf_op jit(solution)/shard_map/all_gather | solution.py:92
  443.1 2.7 convolution_bitcast_fusion
  445.8 1.1 fusion.72
  447.2 0.8 fusion.73
  448.2 53.3 %all-to-all-done.1 = f32[16,1,65536]{2,1,0:T(1,128)} async-done(((f32[16,1,65536]{2,1,0:T(1,128)}), f32[16,1,65536]{2,1,0:T(1,128)}, u32[]{:S(2)}, u32[]{:S(2)}) %all-to-all-start.1) | async-done | bytes 4194336 | tf_op jit(solution)/shard_map/all_to_all | solution.py:80
  501.6 0.5 broadcast.1262
  502.1 13.7 %reduce.68 = f32[16,65536]{1,0:T(8,128)} reduce(f32[16,1,65536]{2,1,0:T(1,128)} %all-to-all-done.1, f32[]{:T(128)} %broadcast.1262), dimensions={1}, to_apply=%all_to_all.25.reduce_sub_computation | reduce | bytes 8388612 | tf_op jit(solution)/shard_map/all_to_all | solution.py:80
  515.8 109.0 %reshape.730 = f32[16384,2,1,4,8]{4,3,2,1,0:T(4,128)} reshape(f32[16,65536]{1,0:T(8,128)} %reduce.68) | data formatting | bytes 8388608
  624.8 53.3 %copy.158 = f32[2,1,4,8,16,1024]{5,3,2,4,0,1:T(8,128)} copy(f32[2,1,4,8,16,1024]{3,2,0,5,4,1:T(4,128)} %bitcast.17) | data formatting | bytes 8388608 | tf_op jit(solution)/shard_map/all_to_all | solution.py:80
  678.1 2.5 copy.141
  681.0 5.3 multiply_subtract_fusion
  686.3 5.3 multiply_add_fusion
  691.7 2.3 pad_maximum_fusion.1
  (41 shorter events, 1.3 us)
Async XLA Ops:
  6.5 8.9 %copy-start.7 = (f32[2,17,16]{1,2,0:T(8,128)S(1)}, f32[2,17,16]{1,2,0:T(8,128)}, u32[]{:S(2)}) copy-start(f32[2,17,16]{1,2,0:T(8,128)} %param.5) | copy-start | bytes 6532
  9.0 49.8 %collective-permute-start = (f32[2,4,8,8192]{3,2,1,0:T(8,128)S(1)}, f32[2,4,8,8192]{3,2,1,0:T(8,128)S(1)}, u32[]{:S(2)}, u32[]{:S(2)}) collective-permute-start(f32[2,4,8,8192]{3,2,1,0:T(8,128)S(1)} %get-tuple-element.75), channel_id=1, source_target_pairs={{0,1},{1,2},{2,3},{4,5},{5,6},{6,7},{8,9},{9,10},{10,11},{12,13},{... | collective-permute-start | bytes 6291464 | tf_op jit(solution)/shard_map/ppermute | solution.py:15
  14.1 50.5 %collective-permute-start.1 = (f32[2,4,8,8192]{3,2,1,0:T(8,128)S(1)}, f32[2,4,8,8192]{3,2,1,0:T(8,128)S(1)}, u32[]{:S(2)}, u32[]{:S(2)}) collective-permute-start(f32[2,4,8,8192]{3,2,1,0:T(8,128)S(1)} %get-tuple-element.76), channel_id=1, source_target_pairs={{1,0},{2,1},{3,2},{5,4},{6,5},{7,6},{9,8},{10,9},{11,10},{13,12},{... | collective-permute-start | bytes 6291464 | tf_op jit(solution)/shard_map/ppermute | solution.py:16
  16.4 44.0 %copy-start = (f32[2,4,16,8192]{3,2,1,0:T(8,128)S(1)}, f32[2,4,16,8192]{3,2,1,0:T(8,128)}, u32[]{:S(2)}) copy-start(f32[2,4,16,8192]{3,2,1,0:T(8,128)} %param.4) | copy-start | bytes 12582916
  162.8 52.6 %all-to-all-start = ((f32[2,4,16,8192]{3,1,0,2:T(4,128)}), f32[2,4,16,8192]{3,1,0,2:T(4,128)}, u32[]{:S(2)}, u32[]{:S(2)}) async-start(f32[2,4,16,8192]{3,1,0,2:T(4,128)} %copy.126), calls=%async_computation | async-start | bytes 8388608 | tf_op jit(solution)/shard_map/all_to_all | solution.py:75
  226.1 4.9 copy-start.2
  235.2 5.4 copy-start.4
  235.2 5.4 copy-start.5
  240.6 3.7 copy-start.3
  247.9 6.2 copy-start.1
  266.3 2.9 copy-start.6
  400.3 42.8 %copy-start.8 = (s32[16]{0:T(128)S(1)}, s32[16]{0:T(128)}, u32[]{:S(2)}) copy-start(s32[16]{0:T(128)} %param.7) | copy-start | bytes 196
  400.3 101.3 %all-to-all-start.1 = ((f32[16,1,65536]{2,1,0:T(1,128)}), f32[16,1,65536]{2,1,0:T(1,128)}, u32[]{:S(2)}, u32[]{:S(2)}) async-start(f32[16,1,65536]{2,1,0:T(1,128)} %reshape.729), calls=%async_computation.1 | async-start | bytes 8388608 | tf_op jit(solution)/shard_map/all_to_all | solution.py:80
  407.3 35.8 %all-gather.2.cloned.1.call-start = ((), (), s32[]{:S(2)}) async-start(), calls=%async_computation.2 | async-start | bytes 3145728 | tf_op jit(solution)/shard_map/all_gather | solution.py:92
Sparse Core Ops, SparseCore 0:
  409.6 33.4 all-gather.1
where the time goes:
time: 714 us; the launch traced here: 701 us
  local copies, waits for them, and re-layouts  331 us (46%)
  waiting for transfers between devices  178 us (25%)
  other arithmetic  123 us (17%)
  matrix products  35.9 us (5%)
  starting transfers between devices  19.2 us (3%)
  between operations  14 us (2%)
    unnamed x37, local copies, waits for them, and re-layouts  193 us
    all_to_all x2, local copies, waits for them, and re-layouts, shards(): lax.all_to_all(spectrum[:, None], ('chan', 'rng'), split_axis=4, concat_a...  53.9 us
    all_to_all x1, waiting for transfers between devices, shards(): lax.all_to_all(spectrum[:, None], ('chan', 'rng'), split_axis=4, concat_a...  53.3 us
    all_to_all x1, waiting for transfers between devices, shards(): lax.all_to_all(filtered, 'az', split_axis=2, concat_axis=3, tiled=True)  46.1 us
    add x1, other arithmetic, shards(): imag_part = imag_part + tap_real * seg_imag + tap_imag * seg_real  44.8 us
    sub x1, other arithmetic, shards(): real_part = real_part + tap_real * seg_real - tap_imag * seg_imag  44.7 us
    mul x1, local copies, waits for them, and re-layouts, azimuth_fft(): jnp.stack([out_real.reshape(lead + (count,)), out_imag.reshape(lead + (co...  44.6 us
    ppermute x1, waiting for transfers between devices, with_halo(): before = lax.ppermute(last, axis, up)  42.5 us
  transfers between devices with their start and end apart: 5, of which 4 were waited for; matrix products, arithmetic and copies ran while one was open for 2% of the time, Pallas kernels for 0%

commit v1 on v0

--- a/solution.py
+++ b/solution.py
@@ -3,6 +3,20 @@
 import jax.numpy as jnp
 from jax import lax
 from jax.sharding import PartitionSpec as P
+
+
+def draft_edges_by_axis(my_tile, array_dim, target):
+    val, y1 = (my_tile.shape[:array_dim], my_tile.shape[array_dim + 1 :])
+    near = my_tile.reshape(*val, target, -1, *y1)
+    part_now = jnp.moveaxis(near, array_dim, 0)
+    return part_now
+
+
+def _convert_sheet(my_data, dim_i):
+    formed = list(my_data.shape[1:])
+    formed[dim_i] *= my_data.shape[0]
+    carry_out = jnp.moveaxis(my_data, 0, dim_i).reshape(formed)
+    return carry_out
 
 
 def with_halo(shard, sides, width):
@@ -58,6 +72,23 @@
 
 
 def shards(raw, taps, recon, channel_slot):
+
+    def answer_series(frame_in, x_part, dev_axis, values):
+        h_now = jax.lax.axis_size(dev_axis)
+        part_next, shaped = (h_now, jax.lax.axis_index(dev_axis))
+        taken_in = draft_edges_by_axis(frame_in, values, part_next)
+        seen_now = taken_in
+        for k0 in range(1, part_next):
+            out_arr, heard = ((shaped + k0) % part_next, (shaped - k0) % part_next)
+            built = lax.dynamic_index_in_dim(taken_in, out_arr, 0)
+            crops = []
+            for t in range(part_next):
+                crops.append((t, (t + k0) % part_next))
+            v_next = jax.lax.ppermute(built, axis_name=dev_axis, perm=crops)
+            seen_now = lax.dynamic_update_slice_in_dim(seen_now, v_next, heard, axis=0)
+        back = _convert_sheet(seen_now, x_part)
+        return back
+
     width = taps.shape[1]
     half = (width - 1) // 2
     strip_rows = raw.shape[2]
@@ -77,9 +108,7 @@
     groups = lax.axis_size("chan")
     local_channels = spectrum.shape[1]
     local_range = spectrum.shape[2]
-    moved = lax.all_to_all(
-        spectrum[:, None], ("chan", "rng"), split_axis=4, concat_axis=1, tiled=True
-    )
+    moved = answer_series(spectrum[:, None], 1, ("chan", "rng"), 4)
     bins = moved.shape[-1]
     moved = moved.reshape((2, groups, strips, local_channels, local_range, bins))
     doppler = jnp.transpose(moved, (0, 1, 3, 2, 4, 5)).reshape(

time: 714 us -> 399 us (0.56); the launches traced: 701 us -> 395 us
  local copies, waits for them, and re-layouts: 331 us -> 55.6 us
  waiting for transfers between devices: 178 us -> 134 us
  starting transfers between devices: 19.2 us -> 49.4 us
  other arithmetic: 123 us -> 107 us
    unnamed x37 -> x65, local copies, waits for them, and re-layouts: 193 us -> 9.28 us
    ppermute x0 -> x15, waiting for transfers between devices: none -> 56.2 us  [answer_series(): v_next = jax.lax.ppermute(built, axis_name=dev_axis, perm=crops)]
    all_to_all x2 -> x0, local copies, waits for them, and re-layouts: 53.9 us -> none  [shards(): lax.all_to_all(spectrum[:, None], ('chan', 'rng'), split_axis=4, concat_a...]
    all_to_all x1 -> x0, waiting for transfers between devices: 53.3 us -> none  [shards(): lax.all_to_all(spectrum[:, None], ('chan', 'rng'), split_axis=4, concat_a...]
    mul x1 -> x0, local copies, waits for them, and re-layouts: 44.6 us -> none  [azimuth_fft(): jnp.stack([out_real.reshape(lead + (count,)), out_imag.reshape(lead + (co...]
    ppermute x0 -> x15, starting transfers between devices: none -> 35.9 us  [answer_series(): v_next = jax.lax.ppermute(built, axis_name=dev_axis, perm=crops)]
    all_gather x1, waiting for transfers between devices: 35.1 us -> 0.02 us  [shards(): piece = lax.all_gather(recon, 'az', axis=1, tiled=True)]
    all_to_all x1 -> x0, other arithmetic: 13.7 us -> none  [shards(): lax.all_to_all(spectrum[:, None], ('chan', 'rng'), split_axis=4, concat_a...]
  transfers between devices with their start and end apart: 5 -> 19, of which waited for: 4 -> 8; matrix products, arithmetic and copies ran while one was open for 2% -> 30% of each run, Pallas kernels for 0% -> 0%
where the time goes in v1:
time: 399 us; the launch traced here: 395 us
  waiting for transfers between devices  134 us (34%)
  other arithmetic  107 us (27%)
  local copies, waits for them, and re-layouts  55.6 us (14%)
  starting transfers between devices  49.4 us (12%)
  matrix products  33.6 us (8%)
  between operations  14.9 us (4%)
    ppermute x15, waiting for transfers between devices, answer_series(): v_next = jax.lax.ppermute(built, axis_name=dev_axis, perm=crops)  56.2 us
    add x1, other arithmetic, shards(): imag_part = imag_part + tap_real * seg_imag + tap_imag * seg_real  44.9 us
    sub x1, other arithmetic, shards(): real_part = real_part + tap_real * seg_real - tap_imag * seg_imag  44.8 us
    ppermute x1, waiting for transfers between devices, with_halo(): before = lax.ppermute(last, axis, up)  40.2 us
    all_to_all x1, waiting for transfers between devices, shards(): lax.all_to_all(filtered, 'az', split_axis=2, concat_axis=3, tiled=True)  37.6 us
    ppermute x15, starting transfers between devices, answer_series(): v_next = jax.lax.ppermute(built, axis_name=dev_axis, perm=crops)  35.9 us
    another operation x4, local copies, waits for them, and re-layouts, azimuth_fft(): jnp.stack([out_real.reshape(lead + (count,)), out_imag.reshape(lead + (co...  10.1 us
    unnamed x65, local copies, waits for them, and re-layouts  9.28 us
  transfers between devices with their start and end apart: 19, of which 8 were waited for; matrix products, arithmetic and copies ran while one was open for 30% of the time, Pallas kernels for 0%

profile of v1, /device:TPU:0, one launch (start us, length us, event | category | flops | bytes accessed | tf_op | source)
XLA Modules:
  0.0 394.5 jit_solution(16569184598536407608)
XLA Ops:
  6.5 4.7 %fusion.72 = (f32[2,4,8,8192]{3,2,1,0:T(8,128)}, f32[2,4,8,8192]{3,2,1,0:T(8,128)}) fusion(f32[2,4,16,8192]{3,2,1,0:T(8,128)} %param.4), kind=kLoop, calls=%fused_computation.217 | loop fusion | bytes 8388608 | tf_op jit(solution)/shard_map/slice | solution.py:27
  11.2 6.3 %collective-permute-start = (f32[2,4,8,8192]{3,2,1,0:T(8,128)}, f32[2,4,8,8192]{3,2,1,0:T(8,128)}, u32[]{:S(2)}, u32[]{:S(2)}) collective-permute-start(f32[2,4,8,8192]{3,2,1,0:T(8,128)} %get-tuple-element.92), channel_id=1, source_target_pairs={{0,1},{1,2},{2,3},{4,5},{5,6},{6,7},{8,9},{9,10},{10,11},{12,13},{... | collective-permute-start | bytes 6291464 | tf_op jit(solution)/shard_map/ppermute | solution.py:29
  17.5 1.3 collective-permute-start.1
  21.1 40.2 %collective-permute-done = f32[2,4,8,8192]{3,2,1,0:T(8,128)} collective-permute-done((f32[2,4,8,8192]{3,2,1,0:T(8,128)}, f32[2,4,8,8192]{3,2,1,0:T(8,128)}, u32[]{:S(2)}, u32[]{:S(2)}) %collective-permute-start) | collective-permute-done | bytes 2097184 | tf_op jit(solution)/shard_map/ppermute | solution.py:29
  61.3 3.1 constant_dynamic-update-slice_fusion.1
  64.4 4.2 %constant_dynamic-update-slice_fusion = (f32[2,4,24,8192]{3,2,1,0:T(8,128)}, f32[2,4,24,8192]{3,2,1,0:T(8,128)}) fusion(f32[2,4,24,8192]{3,2,1,0:T(8,128)} %constant_dynamic-update-slice_fusion.1, f32[2,4,16,8192]{3,2,1,0:T(8,128)S(1)} %copy-done), kind=kLoop, calls=%fused_computation.127 | loop fusion | bytes 12582912 | tf_op jit(solution)/shard_map/concatenate | solution.py:31
  68.6 3.0 constant_dynamic-update-slice_fusion.2
  71.7 44.9 %multiply_add_fusion.2 = f32[1,4,16,8192]{3,2,1,0:T(8,128)} fusion(f32[2,4,24,8192]{3,2,1,0:T(8,128)} %constant_dynamic-update-slice_fusion.2, f32[2,4,24,8192]{3,2,1,0:T(8,128)} %get-tuple-element.90, f32[2,4,16,8192]{3,2,1,0:T(8,128)S(1)} %copy-done, f32[16]{0:T(128)S(1)} %get-tuple-element.37, f32[16]{0:T(128)S(1)} %get-tuple-element.38, ...), kind=kLoop, calls=%fused_computation.10 | loop fusion | flops 35127296 | bytes 73402496 | tf_op jit(solution)/shard_map/add | solution.py:104
  116.6 44.8 %multiply_subtract_fusion.2 = f32[1,4,16,8192]{3,2,1,0:T(8,128)} fusion(f32[2,4,24,8192]{3,2,1,0:T(8,128)} %constant_dynamic-update-slice_fusion.2, f32[2,4,24,8192]{3,2,1,0:T(8,128)} %get-tuple-element.90, f32[2,4,16,8192]{3,2,1,0:T(8,128)S(1)} %copy-done, f32[16]{0:T(128)S(1)} %get-tuple-element.37, f32[16]{0:T(128)S(1)} %get-tuple-element.38, ...), kind=kLoop, calls=%fused_computation.11 | loop fusion | flops 35127296 | bytes 73402496 | tf_op jit(solution)/shard_map/sub | solution.py:103
  161.4 2.5 pad_maximum_fusion
  163.9 4.7 %copy.76 = f32[2,4,16,8192]{3,1,0,2:T(4,128)} copy(f32[2,4,16,8192]{3,2,1,0:T(8,128)S(1)} %pad_maximum_fusion) | data formatting | bytes 8388608 | tf_op jit(solution)/shard_map/stack | solution.py:105
  168.6 6.0 %all-to-all-start = ((f32[2,4,16,8192]{3,1,0,2:T(4,128)}), f32[2,4,16,8192]{3,1,0,2:T(4,128)}, u32[]{:S(2)}, u32[]{:S(2)}) async-start(f32[2,4,16,8192]{3,1,0,2:T(4,128)} %copy.76), calls=%async_computation | async-start | bytes 8388608 | tf_op jit(solution)/shard_map/all_to_all | solution.py:106
  174.6 2.7 convolution_bitcast_fusion
  177.4 1.5 fusion.73
  179.2 1.3 fusion.74
  183.8 37.6 %all-to-all-done = f32[2,4,16,8192]{3,1,0,2:T(4,128)} async-done(((f32[2,4,16,8192]{3,1,0,2:T(4,128)}), f32[2,4,16,8192]{3,1,0,2:T(4,128)}, u32[]{:S(2)}, u32[]{:S(2)}) %all-to-all-start) | async-done | bytes 4194336 | tf_op jit(solution)/shard_map/all_to_all | solution.py:106
  221.4 5.4 %copy.171 = f32[2,4,2,8,8192]{4,2,3,1,0:T(2,128)S(1)} copy(f32[2,4,2,8,8192]{4,1,0,3,2:T(4,128)} %bitcast.5) | data formatting | bytes 8388608 | tf_op jit(solution)/shard_map/all_to_all | solution.py:106
  226.8 2.3 fusion.71
  229.1 3.1 reshape_squeeze.6
  232.2 4.8 %fusion.8 = f32[4,8,128,128]{3,2,1,0:T(8,128)} fusion(f32[4,8,128,128]{3,2,1,0:T(8,128)S(1)} %reshape_squeeze.6), kind=kOutput, calls=%fused_computation.107 | convolution fusion | flops 805535744 | bytes 4194304 | tf_op jit(solution)/shard_map/...ab,af->...bf/dot_general | solution.py:54
  237.0 3.5 reshape_squeeze.7
  240.5 1.3 copy-done.5
  241.8 3.6 fusion.6
  245.5 5.3 %convolution_add_fusion = f32[4,8,128,128]{3,2,1,0:T(8,128)S(1)} fusion(f32[4,8,128,128]{3,2,1,0:T(8,128)S(1)} %copy-done.6, f32[4,8,128,128]{3,2,1,0:T(8,128)} %copy-done.5), kind=kOutput, calls=%fused_computation.14 | convolution fusion | flops 806060032 | bytes 6291456 | tf_op jit(solution)/shard_map/...ab,af->...bf/dot_general | solution.py:54
  250.8 3.6 convolution_subtract_fusion
  254.4 2.5 fusion.1
  256.9 3.6 fusion
  260.5 3.7 subtract_bitcast_fusion
  264.2 2.7 stack.19
  266.9 4.3 %copy.89 = f32[1,1,4,8,16,1024]{5,3,2,4,0,1:T(8,128)} copy(f32[1,1,4,8,16,1024]{5,4,3,2,1,0:T(8,128)} %stack.19) | data formatting | bytes 4194304 | tf_op jit(solution)/shard_map/stack | solution.py:71
  271.2 3.7 add_bitcast_fusion
  274.9 1.9 stack.18
  278.4 1.4 maximum_multiply_fusion
  280.3 2.5 collective-permute-start.2
  282.8 2.6 collective-permute-start.3
  285.5 2.2 collective-permute-start.5
  288.3 2.2 collective-permute-done.2
  290.6 13.5 %collective-permute-done.3 = f32[1,2,1,4,8,1024]{5,4,3,0,1,2:T(8,128)S(1)} collective-permute-done((f32[1,2,1,4,8,1024]{5,4,3,0,1,2:T(8,128)S(1)}, f32[1,2,1,4,8,1024]{5,4,3,0,1,2:T(8,128)S(1)}, u32[]{:S(2)}, u32[]{:S(2)}) %collective-permute-start.3) | collective-permute-done | bytes 262176 | tf_op jit(solution)/shard_map/ppermute | solution.py:87
  305.0 1.4 collective-permute-start.9
  306.5 18.2 %collective-permute-start.10 = (f32[1,2,1,4,8,1024]{5,4,3,0,1,2:T(8,128)S(1)}, f32[1,2,1,4,8,1024]{5,4,3,0,1,2:T(8,128)S(1)}, u32[]{:S(2)}, u32[]{:S(2)}) collective-permute-start(f32[1,2,1,4,8,1024]{5,4,3,0,1,2:T(8,128)S(1)} %get-tuple-element.77), channel_id=1, source_target_pairs={{0,17},{1,18},{2,19},{3,24},{8,25},{9,26},{10,27},{11,0},{16,1},{1... | collective-permute-start | bytes 786440 | tf_op jit(solution)/shard_map/ppermute | solution.py:87
  324.8 11.9 %collective-permute-done.7 = f32[1,2,1,4,8,1024]{5,4,3,0,1,2:T(8,128)S(1)} collective-permute-done((f32[1,2,1,4,8,1024]{5,4,3,0,1,2:T(8,128)S(1)}, f32[1,2,1,4,8,1024]{5,4,3,0,1,2:T(8,128)S(1)}, u32[]{:S(2)}, u32[]{:S(2)}) %collective-permute-start.7) | collective-permute-done | bytes 262176 | tf_op jit(solution)/shard_map/ppermute | solution.py:87
  338.0 6.1 %collective-permute-start.14 = (f32[1,2,1,4,8,1024]{5,4,3,0,1,2:T(8,128)S(1)}, f32[1,2,1,4,8,1024]{5,4,3,0,1,2:T(8,128)S(1)}, u32[]{:S(2)}, u32[]{:S(2)}) collective-permute-start(f32[1,2,1,4,8,1024]{5,4,3,0,1,2:T(8,128)S(1)} %get-tuple-element.73), channel_id=1, source_target_pairs={{0,25},{1,26},{2,27},{3,0},{8,1},{9,2},{10,3},{11,8},{16,9},{17,10... | collective-permute-start | bytes 786440 | tf_op jit(solution)/shard_map/ppermute | solution.py:87
  344.2 15.2 %collective-permute-done.11 = f32[1,2,1,4,8,1024]{5,4,3,0,1,2:T(8,128)S(1)} collective-permute-done((f32[1,2,1,4,8,1024]{5,4,3,0,1,2:T(8,128)S(1)}, f32[1,2,1,4,8,1024]{5,4,3,0,1,2:T(8,128)S(1)}, u32[]{:S(2)}, u32[]{:S(2)}) %collective-permute-start.11) | collective-permute-done | bytes 262176 | tf_op jit(solution)/shard_map/ppermute | solution.py:87
  359.5 11.1 %collective-permute-done.15 = f32[1,2,1,4,8,1024]{5,4,3,0,1,2:T(8,128)S(1)} collective-permute-done((f32[1,2,1,4,8,1024]{5,4,3,0,1,2:T(8,128)S(1)}, f32[1,2,1,4,8,1024]{5,4,3,0,1,2:T(8,128)S(1)}, u32[]{:S(2)}, u32[]{:S(2)}) %collective-permute-start.15) | collective-permute-done | bytes 262176 | tf_op jit(solution)/shard_map/ppermute | solution.py:87
  370.6 2.3 collective-permute-done.16
  374.6 5.2 %multiply_add_fusion = f32[1,16,4,8,1024]{4,3,2,1,0:T(8,128)S(1)} fusion(f32[4,8,1024]{2,1,0:T(8,128)S(1)} %get-tuple-element.40, f32[16,1024]{1,0:T(8,128)S(1)} %get-tuple-element.126, f32[4,8,1024]{2,1,0:T(8,128)S(1)} %get-tuple-element.41, f32[16,1024]{1,0:T(8,128)S(1)} %get-tuple-element.127, f32[4,8,1024]{2,1,0:T(8,128)S(1)} %get-tuple-element.42, ...), kind=kLoop, calls=%fused_computation.4 | loop fusion | flops 33030144 | bytes 8388608 | tf_op jit(solution)/shard_map/add | solution.py:132
  379.8 5.3 %multiply_subtract_fusion = f32[1,16,4,8,1024]{4,3,2,1,0:T(8,128)S(1)} fusion(f32[4,8,1024]{2,1,0:T(8,128)S(1)} %get-tuple-element.40, f32[16,1024]{1,0:T(8,128)S(1)} %get-tuple-element.126, f32[4,8,1024]{2,1,0:T(8,128)S(1)} %get-tuple-element.41, f32[16,1024]{1,0:T(8,128)S(1)} %get-tuple-element.127, f32[4,8,1024]{2,1,0:T(8,128)S(1)} %get-tuple-element.42, ...), kind=kLoop, calls=%fused_computation.5 | loop fusion | flops 33030144 | bytes 8388608 | tf_op jit(solution)/shard_map/sub | solution.py:131
  385.1 2.3 pad_maximum_fusion.1
  (111 shorter events, 12.0 us)
Async XLA Ops:
  6.5 12.5 %copy-start.9 = (f32[2,17,16]{1,2,0:T(8,128)S(1)}, f32[2,17,16]{1,2,0:T(8,128)}, u32[]{:S(2)}) copy-start(f32[2,17,16]{1,2,0:T(8,128)} %param.5) | copy-start | bytes 6532
  6.5 168.1 %all-gather.2.cloned.1.call-start = ((), (), s32[]{:S(2)}) async-start(), calls=%async_computation.1 | async-start | bytes 3145728 | tf_op jit(solution)/shard_map/all_gather | solution.py:121
  11.2 50.1 %collective-permute-start = (f32[2,4,8,8192]{3,2,1,0:T(8,128)}, f32[2,4,8,8192]{3,2,1,0:T(8,128)}, u32[]{:S(2)}, u32[]{:S(2)}) collective-permute-start(f32[2,4,8,8192]{3,2,1,0:T(8,128)} %get-tuple-element.92), channel_id=1, source_target_pairs={{0,1},{1,2},{2,3},{4,5},{5,6},{6,7},{8,9},{9,10},{10,11},{12,13},{... | collective-permute-start | bytes 6291464 | tf_op jit(solution)/shard_map/ppermute | solution.py:29
  17.5 51.1 %collective-permute-start.1 = (f32[2,4,8,8192]{3,2,1,0:T(8,128)}, f32[2,4,8,8192]{3,2,1,0:T(8,128)}, u32[]{:S(2)}, u32[]{:S(2)}) collective-permute-start(f32[2,4,8,8192]{3,2,1,0:T(8,128)} %get-tuple-element.93), channel_id=1, source_target_pairs={{1,0},{2,1},{3,2},{5,4},{6,5},{7,6},{9,8},{10,9},{11,10},{13,12},{... | collective-permute-start | bytes 6291464 | tf_op jit(solution)/shard_map/ppermute | solution.py:30
  21.1 43.3 %copy-start = (f32[2,4,16,8192]{3,2,1,0:T(8,128)S(1)}, f32[2,4,16,8192]{3,2,1,0:T(8,128)}, u32[]{:S(2)}) copy-start(f32[2,4,16,8192]{3,2,1,0:T(8,128)} %param.4) | copy-start | bytes 12582916
  168.6 6.0 %copy-start.23 = (s32[16]{0:T(128)S(1)}, s32[16]{0:T(128)}, u32[]{:S(2)}) copy-start(s32[16]{0:T(128)} %param.7) | copy-start | bytes 196
  168.6 52.8 %all-to-all-start = ((f32[2,4,16,8192]{3,1,0,2:T(4,128)}), f32[2,4,16,8192]{3,1,0,2:T(4,128)}, u32[]{:S(2)}, u32[]{:S(2)}) async-start(f32[2,4,16,8192]{3,1,0,2:T(4,128)} %copy.76), calls=%async_computation | async-start | bytes 8388608 | tf_op jit(solution)/shard_map/all_to_all | solution.py:106
  232.2 4.9 %copy-start.3 = (f32[4,8,128,128]{3,2,1,0:T(8,128)}, f32[4,8,128,128]{3,2,1,0:T(8,128)S(1)}, u32[]{:S(2)}) copy-start(f32[4,8,128,128]{3,2,1,0:T(8,128)S(1)} %reshape_squeeze.6) | copy-start | bytes 6291460
  240.5 1.3 copy-start.5
  241.8 3.6 copy-start.6
  245.5 5.3 %copy-start.4 = (f32[4,8,128,128]{3,2,1,0:T(8,128)S(1)}, f32[4,8,128,128]{3,2,1,0:T(8,128)}, u32[]{:S(2)}) copy-start(f32[4,8,128,128]{3,2,1,0:T(8,128)} %copy-done.3) | copy-start | bytes 6291460
  254.4 6.1 %copy-start.1 = (f32[4,8,128,128]{3,2,1,0:T(8,128)}, f32[4,8,128,128]{3,2,1,0:T(8,128)S(1)}, u32[]{:S(2)}) copy-start(f32[4,8,128,128]{3,2,1,0:T(8,128)S(1)} %convolution_subtract_fusion) | copy-start | bytes 6291460
  266.9 4.3 %copy-start.2 = (f32[4,8,128,128]{3,2,1,0:T(8,128)S(1)}, f32[4,8,128,128]{3,2,1,0:T(8,128)}, u32[]{:S(2)}) copy-start(f32[4,8,128,128]{3,2,1,0:T(8,128)} %copy-done.1) | copy-start | bytes 6291460
  266.9 4.3 %copy-start.7 = (f32[128,4,8,128]{3,0,2,1:T(8,128)S(1)}, f32[128,4,8,128]{3,0,2,1:T(8,128)}, u32[]{:S(2)}) copy-start(f32[128,4,8,128]{3,0,2,1:T(8,128)} %fusion) | copy-start | bytes 6291460
  276.8 1.6 copy-start.8
  279.9 3.0 copy-start.21
  279.9 3.0 copy-start.22
  279.9 5.6 %copy-start.19 = (f32[1,16,1,1024]{3,2,1,0:T(1,128)S(1)}, f32[1,16,1,1024]{3,2,1,0:T(1,128)}, u32[]{:S(2)}) copy-start(f32[1,16,1,1024]{3,2,1,0:T(1,128)} %get-tuple-element.94) | copy-start | bytes 196612
  279.9 5.6 %copy-start.20 = (f32[1,16,1,1024]{3,2,1,0:T(1,128)S(1)}, f32[1,16,1,1024]{3,2,1,0:T(1,128)}, u32[]{:S(2)}) copy-start(f32[1,16,1,1024]{3,2,1,0:T(1,128)} %get-tuple-element.113) | copy-start | bytes 196612
  280.3 10.3 %collective-permute-start.2 = (f32[1,2,1,4,8,1024]{5,4,3,0,1,2:T(8,128)S(1)}, f32[1,2,1,4,8,1024]{5,4,3,0,1,2:T(8,128)S(1)}, u32[]{:S(2)}, u32[]{:S(2)}) collective-permute-start(f32[1,2,1,4,8,1024]{5,4,3,0,1,2:T(8,128)S(1)} %get-tuple-element.85), channel_id=1, source_target_pairs={{0,1},{1,2},{2,3},{3,8},{8,9},{9,10},{10,11},{11,16},{16,17},{17,1... | collective-permute-start | bytes 786440 | tf_op jit(solution)/shard_map/ppermute | solution.py:87
  282.8 21.3 %collective-permute-start.3 = (f32[1,2,1,4,8,1024]{5,4,3,0,1,2:T(8,128)S(1)}, f32[1,2,1,4,8,1024]{5,4,3,0,1,2:T(8,128)S(1)}, u32[]{:S(2)}, u32[]{:S(2)}) collective-permute-start(f32[1,2,1,4,8,1024]{5,4,3,0,1,2:T(8,128)S(1)} %get-tuple-element.84), channel_id=1, source_target_pairs={{0,2},{1,3},{2,8},{3,9},{8,10},{9,11},{10,16},{11,17},{16,18},{17,... | collective-permute-start | bytes 786440 | tf_op jit(solution)/shard_map/ppermute | solution.py:87
  285.5 19.5 %collective-permute-start.4 = (f32[1,2,1,4,8,1024]{5,4,3,0,1,2:T(8,128)S(1)}, f32[1,2,1,4,8,1024]{5,4,3,0,1,2:T(8,128)S(1)}, u32[]{:S(2)}, u32[]{:S(2)}) collective-permute-start(f32[1,2,1,4,8,1024]{5,4,3,0,1,2:T(8,128)S(1)} %get-tuple-element.83), channel_id=1, source_target_pairs={{0,3},{1,8},{2,9},{3,10},{8,11},{9,16},{10,17},{11,18},{16,19},{17... | collective-permute-start | bytes 786440 | tf_op jit(solution)/shard_map/ppermute | solution.py:87
  285.5 20.9 %collective-permute-start.5 = (f32[1,2,1,4,8,1024]{5,4,3,0,1,2:T(8,128)S(1)}, f32[1,2,1,4,8,1024]{5,4,3,0,1,2:T(8,128)S(1)}, u32[]{:S(2)}, u32[]{:S(2)}) collective-permute-start(f32[1,2,1,4,8,1024]{5,4,3,0,1,2:T(8,128)S(1)} %get-tuple-element.82), channel_id=1, source_target_pairs={{0,8},{1,9},{2,10},{3,11},{8,16},{9,17},{10,18},{11,19},{16,24},{1... | collective-permute-start | bytes 786440 | tf_op jit(solution)/shard_map/ppermute | solution.py:87
  287.7 37.0 %collective-permute-start.6 = (f32[1,2,1,4,8,1024]{5,4,3,0,1,2:T(8,128)S(1)}, f32[1,2,1,4,8,1024]{5,4,3,0,1,2:T(8,128)S(1)}, u32[]{:S(2)}, u32[]{:S(2)}) collective-permute-start(f32[1,2,1,4,8,1024]{5,4,3,0,1,2:T(8,128)S(1)} %get-tuple-element.81), channel_id=1, source_target_pairs={{0,9},{1,10},{2,11},{3,16},{8,17},{9,18},{10,19},{11,24},{16,25},{... | collective-permute-start | bytes 786440 | tf_op jit(solution)/shard_map/ppermute | solution.py:87
  290.5 46.2 %collective-permute-start.7 = (f32[1,2,1,4,8,1024]{5,4,3,0,1,2:T(8,128)S(1)}, f32[1,2,1,4,8,1024]{5,4,3,0,1,2:T(8,128)S(1)}, u32[]{:S(2)}, u32[]{:S(2)}) collective-permute-start(f32[1,2,1,4,8,1024]{5,4,3,0,1,2:T(8,128)S(1)} %get-tuple-element.80), channel_id=1, source_target_pairs={{0,10},{1,11},{2,16},{3,17},{8,18},{9,19},{10,24},{11,25},{16,26},... | collective-permute-start | bytes 786440 | tf_op jit(solution)/shard_map/ppermute | solution.py:87
  304.1 32.6 %collective-permute-start.8 = (f32[1,2,1,4,8,1024]{5,4,3,0,1,2:T(8,128)S(1)}, f32[1,2,1,4,8,1024]{5,4,3,0,1,2:T(8,128)S(1)}, u32[]{:S(2)}, u32[]{:S(2)}) collective-permute-start(f32[1,2,1,4,8,1024]{5,4,3,0,1,2:T(8,128)S(1)} %get-tuple-element.79), channel_id=1, source_target_pairs={{0,11},{1,16},{2,17},{3,18},{8,19},{9,24},{10,25},{11,26},{16,27},... | collective-permute-start | bytes 786440 | tf_op jit(solution)/shard_map/ppermute | solution.py:87
  305.0 32.9 %collective-permute-start.9 = (f32[1,2,1,4,8,1024]{5,4,3,0,1,2:T(8,128)S(1)}, f32[1,2,1,4,8,1024]{5,4,3,0,1,2:T(8,128)S(1)}, u32[]{:S(2)}, u32[]{:S(2)}) collective-permute-start(f32[1,2,1,4,8,1024]{5,4,3,0,1,2:T(8,128)S(1)} %get-tuple-element.78), channel_id=1, source_target_pairs={{0,16},{1,17},{2,18},{3,19},{8,24},{9,25},{10,26},{11,27},{16,0},{... | collective-permute-start | bytes 786440 | tf_op jit(solution)/shard_map/ppermute | solution.py:87
  306.5 37.6 %collective-permute-start.10 = (f32[1,2,1,4,8,1024]{5,4,3,0,1,2:T(8,128)S(1)}, f32[1,2,1,4,8,1024]{5,4,3,0,1,2:T(8,128)S(1)}, u32[]{:S(2)}, u32[]{:S(2)}) collective-permute-start(f32[1,2,1,4,8,1024]{5,4,3,0,1,2:T(8,128)S(1)} %get-tuple-element.77), channel_id=1, source_target_pairs={{0,17},{1,18},{2,19},{3,24},{8,25},{9,26},{10,27},{11,0},{16,1},{1... | collective-permute-start | bytes 786440 | tf_op jit(solution)/shard_map/ppermute | solution.py:87
  324.7 34.7 %collective-permute-start.11 = (f32[1,2,1,4,8,1024]{5,4,3,0,1,2:T(8,128)S(1)}, f32[1,2,1,4,8,1024]{5,4,3,0,1,2:T(8,128)S(1)}, u32[]{:S(2)}, u32[]{:S(2)}) collective-permute-start(f32[1,2,1,4,8,1024]{5,4,3,0,1,2:T(8,128)S(1)} %get-tuple-element.76), channel_id=1, source_target_pairs={{0,18},{1,19},{2,24},{3,25},{8,26},{9,27},{10,0},{11,1},{16,2},{17... | collective-permute-start | bytes 786440 | tf_op jit(solution)/shard_map/ppermute | solution.py:87
  336.7 22.7 %collective-permute-start.12 = (f32[1,2,1,4,8,1024]{5,4,3,0,1,2:T(8,128)S(1)}, f32[1,2,1,4,8,1024]{5,4,3,0,1,2:T(8,128)S(1)}, u32[]{:S(2)}, u32[]{:S(2)}) collective-permute-start(f32[1,2,1,4,8,1024]{5,4,3,0,1,2:T(8,128)S(1)} %get-tuple-element.75), channel_id=1, source_target_pairs={{0,19},{1,24},{2,25},{3,26},{8,27},{9,0},{10,1},{11,2},{16,3},{17,... | collective-permute-start | bytes 786440 | tf_op jit(solution)/shard_map/ppermute | solution.py:87
  336.8 22.7 %collective-permute-start.13 = (f32[1,2,1,4,8,1024]{5,4,3,0,1,2:T(8,128)S(1)}, f32[1,2,1,4,8,1024]{5,4,3,0,1,2:T(8,128)S(1)}, u32[]{:S(2)}, u32[]{:S(2)}) collective-permute-start(f32[1,2,1,4,8,1024]{5,4,3,0,1,2:T(8,128)S(1)} %get-tuple-element.74), channel_id=1, source_target_pairs={{0,24},{1,25},{2,26},{3,27},{8,0},{9,1},{10,2},{11,3},{16,8},{17,9... | collective-permute-start | bytes 786440 | tf_op jit(solution)/shard_map/ppermute | solution.py:87
  338.0 21.5 %collective-permute-start.14 = (f32[1,2,1,4,8,1024]{5,4,3,0,1,2:T(8,128)S(1)}, f32[1,2,1,4,8,1024]{5,4,3,0,1,2:T(8,128)S(1)}, u32[]{:S(2)}, u32[]{:S(2)}) collective-permute-start(f32[1,2,1,4,8,1024]{5,4,3,0,1,2:T(8,128)S(1)} %get-tuple-element.73), channel_id=1, source_target_pairs={{0,25},{1,26},{2,27},{3,0},{8,1},{9,2},{10,3},{11,8},{16,9},{17,10... | collective-permute-start | bytes 786440 | tf_op jit(solution)/shard_map/ppermute | solution.py:87
  344.1 26.5 %collective-permute-start.15 = (f32[1,2,1,4,8,1024]{5,4,3,0,1,2:T(8,128)S(1)}, f32[1,2,1,4,8,1024]{5,4,3,0,1,2:T(8,128)S(1)}, u32[]{:S(2)}, u32[]{:S(2)}) collective-permute-start(f32[1,2,1,4,8,1024]{5,4,3,0,1,2:T(8,128)S(1)} %get-tuple-element.72), channel_id=1, source_target_pairs={{0,26},{1,27},{2,0},{3,1},{8,2},{9,3},{10,8},{11,9},{16,10},{17,11... | collective-permute-start | bytes 786440 | tf_op jit(solution)/shard_map/ppermute | solution.py:87
  359.4 13.6 %collective-permute-start.16 = (f32[1,2,1,4,8,1024]{5,4,3,0,1,2:T(8,128)S(1)}, f32[1,2,1,4,8,1024]{5,4,3,0,1,2:T(8,128)S(1)}, u32[]{:S(2)}, u32[]{:S(2)}) collective-permute-start(f32[1,2,1,4,8,1024]{5,4,3,0,1,2:T(8,128)S(1)} %get-tuple-element.71), channel_id=1, source_target_pairs={{0,27},{1,0},{2,1},{3,2},{8,3},{9,8},{10,9},{11,10},{16,11},{17,16... | collective-permute-start | bytes 786440 | tf_op jit(solution)/shard_map/ppermute | solution.py:87
  373.5 0.8 copy-start.10
  373.5 0.9 copy-start.11
  373.5 0.9 copy-start.12
  373.5 0.9 copy-start.13
  373.5 0.9 copy-start.14
  373.5 1.0 copy-start.15
  373.5 1.0 copy-start.16
  373.5 1.0 copy-start.17
  373.5 1.0 copy-start.18
Sparse Core Ops, SparseCore 0:
  18.9 35.4 all-gather.1
